TPU v7x, 32 devices: a whole 2x2x4 slice. The times are simulated.
32 devices in a mesh: slab: 8 (over z, x), pencil: 4 (over y, core).
Axes of the slice: x: 2, y: 2, z: 4, core: 2. Of those that a mesh axis runs over, the one named last changes fastest.
Arguments:
- atom_cell: int32 [3, 262144], P(None, ('slab', 'pencil')), may hold values from 0 to 511, as said below
- charge: float32 [262144], P(('slab', 'pencil')), may hold values from -4 to 4
Outputs:
- potential: float32 [64, 128, 512], P('slab', 'pencil')
- forces: float32 [3, 262144], P(None, ('slab', 'pencil'))
Inputs may be any that keep to these rules, and one draw needn't show every extreme that they name: `atom_cell`: the atoms of rows b * 8192 to (b + 1) * 8192 - 1, with b = s * 4 + r, lie in z planes s * 8 to (s + 1) * 8 - 1 and y rows r * 32 to (r + 1) * 32 - 1. Row 0 is at cell (0, 0, 0) and the last row at cell (63, 127, 511).
All inputs are finite; a program needn't handle non-finite values.
Results may differ from a plain program's by a relative error of at most 0.0003.
Values sent between devices are 32-bit elements; how exact they have to be, the bound alone decides.
A program may use at most 128 MiB of HBM per device.

v0:
```python
from functools import partial
import math
import jax
import jax.numpy as jnp
from jax import lax
from jax.sharding import PartitionSpec as P

CZ = 8
CY = 32
NX = 512
LEVELS = 5
RADIUS = 2
F = 32


def extended(cells, sides, width):
    for axis, dim in sides:
        count = lax.axis_size(axis)
        ends = count - 1
        head = lax.slice_in_dim(cells, 0, width, axis=dim)
        tail = lax.slice_in_dim(cells, cells.shape[dim] - width, cells.shape[dim], axis=dim)
        cells = jnp.concatenate(
            [
                lax.ppermute(tail, axis, [(i, (i + 1) % count) for i in range(ends)]),
                cells,
                lax.ppermute(head, axis, [((i + 1) % count, i) for i in range(ends)]),
            ],
            axis=dim,
        )
    return cells


def kernel_weight(step_z, step_y, step_x):
    squared = step_z * step_z + step_y * step_y + step_x * step_x
    return 1.0 / math.sqrt(squared + 0.25) - 1.0 / math.sqrt(squared + 4.0)


def level_weight(scale, step_z, step_y, step_x):
    squared = step_z * step_z + step_y * step_y + step_x * step_x
    return scale * (1.0 / math.sqrt(squared + 1.0) - 1.0 / math.sqrt(squared + 4.0))


def short_field(padded, plane_count, row_count, row_length, radius_cells, weight_of):
    accumulated = jnp.zeros((plane_count, row_count, row_length), jnp.float32)
    for step_z in range(-radius_cells, radius_cells + 1):
        for step_y in range(-radius_cells, radius_cells + 1):
            for step_x in range(-radius_cells, radius_cells + 1):
                corner_z = radius_cells + step_z
                corner_y = radius_cells + step_y
                corner_x = radius_cells + step_x
                accumulated = (
                    accumulated
                    + weight_of(step_z, step_y, step_x)
                    * padded[
                        corner_z : corner_z + plane_count,
                        corner_y : corner_y + row_count,
                        corner_x : corner_x + row_length,
                    ]
                )
    return accumulated


def restrict(grid):
    planes, rows, length = grid.shape
    return grid.reshape(planes // 2, 2, rows // 2, 2, length // 2, 2).sum(axis=(1, 3, 5))


def restrict_plane(plane):
    rows, length = plane.shape
    return plane.reshape(rows // 2, 2, length // 2, 2).sum(axis=(1, 3))


def interp_matrix(fine_ids, level_count, factor, first_col, width):
    numerator = jnp.clip(2 * fine_ids + 1 - factor, 0, 2 * factor * (level_count - 1))
    lower_index = jnp.minimum(numerator // (2 * factor), level_count - 2)
    fraction = (numerator - lower_index * 2 * factor).astype(jnp.float32) / (2.0 * factor)
    local_index = lower_index - first_col
    columns = jnp.arange(width, dtype=jnp.int32)
    low_part = jnp.where(columns[None, :] == local_index[:, None], 1.0 - fraction[:, None], 0.0)
    high_part = jnp.where(columns[None, :] == local_index[:, None] + 1, fraction[:, None], 0.0)
    return low_part + high_part


def to_fine(field, counts, factor, plane_ids, line_ids, column_ids, first_z, first_y):
    width_z, width_y, width_x = field.shape
    along_z = interp_matrix(plane_ids, counts[0], factor, first_z, width_z)
    along_y = interp_matrix(line_ids, counts[1], factor, first_y, width_y)
    along_x = interp_matrix(column_ids, counts[2], factor, 0, width_x)
    section = jnp.einsum("fa,abc->fbc", along_z, field, precision=lax.Precision.HIGHEST)
    section = jnp.einsum("fb,abc->afc", along_y, section, precision=lax.Precision.HIGHEST)
    return jnp.einsum("fc,abc->abf", along_x, section, precision=lax.Precision.HIGHEST)


def top_coords(cell_ids, top_y, top_x):
    return (cell_ids // (top_y * top_x), cell_ids // top_x % top_y, cell_ids % top_x)


def top_potential(targets, charges_flat, top_z, top_y, top_x, strength):
    sources = jnp.arange(top_z * top_y * top_x, dtype=jnp.int32)
    target_xyz = top_coords(targets, top_y, top_x)
    source_xyz = top_coords(sources, top_y, top_x)
    distance = jnp.ones((targets.shape[0], sources.shape[0]), jnp.float32)
    for component in range(3):
        offset = (target_xyz[component][:, None] - source_xyz[component][None, :]).astype(
            jnp.float32
        )
        distance = distance + offset * offset
    kernel = strength / jnp.sqrt(distance)
    return jnp.dot(kernel, charges_flat, precision=lax.Precision.HIGHEST)


def gradient_along(padded, direction, plane_count, row_count, row_length):

    def shifted(offset_cells):
        corner = [2, 2, 2]
        corner[direction] = corner[direction] + offset_cells
        return padded[
            corner[0] : corner[0] + plane_count,
            corner[1] : corner[1] + row_count,
            corner[2] : corner[2] + row_length,
        ]

    return (8.0 * (shifted(1) - shifted(-1)) - (shifted(2) - shifted(-2))) / 12.0


def body(atom_cell, charge):
    slab_pos = lax.axis_index("slab")
    pencil_pos = lax.axis_index("pencil")
    slabs = lax.axis_size("slab")
    pencils = lax.axis_size("pencil")
    atom_total = charge.shape[0]
    row_cells = CZ * CY
    plane_row = (atom_cell[0] - slab_pos * CZ) * CY + (atom_cell[1] - pencil_pos * CY)
    column_of = atom_cell[2]
    block_atoms = math.gcd(atom_total, 512)
    block_count = atom_total // block_atoms
    row_blocks = plane_row.reshape(block_count, block_atoms)
    column_blocks = column_of.reshape(block_count, block_atoms)
    charge_blocks = charge.reshape(block_count, block_atoms)
    row_range = jnp.arange(row_cells, dtype=jnp.int32)
    column_range = jnp.arange(NX, dtype=jnp.int32)

    def deposit(total, block):
        rows_here, columns_here, charges_here = block
        row_table = (rows_here[:, None] == row_range[None, :]).astype(jnp.float32)
        column_table = jnp.where(
            columns_here[:, None] == column_range[None, :], charges_here[:, None], 0.0
        )
        added = jnp.dot(row_table.T, column_table, precision=lax.Precision.HIGHEST)
        return (total + added, None)

    charge_grid, _ = lax.scan(
        deposit, jnp.zeros((row_cells, NX), jnp.float32), (row_blocks, column_blocks, charge_blocks)
    )
    charge_grid = charge_grid.reshape(CZ, CY, NX)
    plane_ids = slab_pos * CZ + jnp.arange(CZ, dtype=jnp.int32)
    line_ids = pencil_pos * CY + jnp.arange(CY, dtype=jnp.int32)
    column_ids = jnp.arange(NX, dtype=jnp.int32)
    plane_level = CZ.bit_length() - 1
    rimmed = extended(charge_grid, (("slab", 0), ("pencil", 1)), RADIUS)
    padded = jnp.pad(rimmed, ((0, 0), (0, 0), (RADIUS, RADIUS)))
    potential = short_field(padded, CZ, CY, NX, RADIUS, kernel_weight)
    level_charge = charge_grid
    for level in range(1, plane_level):
        level_charge = restrict(level_charge)
        level_z, level_y, level_x = level_charge.shape
        cycle = extended(level_charge, (("slab", 0), ("pencil", 1)), RADIUS)
        cycle = jnp.pad(cycle, ((0, 0), (0, 0), (RADIUS, RADIUS)))
        field = short_field(
            cycle, level_z, level_y, level_x, RADIUS, partial(level_weight, 1.0 / 2**level)
        )
        framed = extended(field, (("slab", 0), ("pencil", 1)), 1)
        counts = (level_z * slabs, level_y * pencils, level_x)
        potential = potential + to_fine(
            framed,
            counts,
            2**level,
            plane_ids,
            line_ids,
            column_ids,
            slab_pos * level_z - 1,
            pencil_pos * level_y - 1,
        )
    own_plane = restrict(level_charge)[0]
    pieces = [own_plane]
    partial_plane = own_plane
    for level_bit in range(LEVELS - plane_level):
        partial_plane = restrict_plane(partial_plane)
        pieces.append(partial_plane)
    packed = jnp.concatenate([piece.reshape(1, -1) for piece in pieces], axis=1)
    gathered = lax.all_gather(packed, ("slab", "pencil"), axis=0, tiled=True)
    coarse = []
    offset = 0
    for step, piece in enumerate(pieces):
        rows, length = piece.shape
        group = 2**step
        block = gathered[:, offset : offset + rows * length].reshape(
            slabs // group, group, pencils, rows, length
        )
        grid = block.sum(axis=1)
        coarse.append(grid.reshape(slabs // group, pencils * rows, length))
        offset = offset + rows * length
    for step in range(LEVELS - plane_level):
        level = plane_level + step
        grid = coarse[step]
        level_z, level_y, level_x = grid.shape
        field = short_field(
            jnp.pad(grid, RADIUS),
            level_z,
            level_y,
            level_x,
            RADIUS,
            partial(level_weight, 1.0 / 2**level),
        )
        potential = potential + to_fine(
            field, field.shape, 2**level, plane_ids, line_ids, column_ids, 0, 0
        )
    top_grid = coarse[-1]
    top_z, top_y, top_x = top_grid.shape
    charges_flat = top_grid.reshape(top_z * top_y * top_x)
    top_total = top_z * top_y * top_x
    strength = 1.0 / F
    block_rows = math.gcd(top_total, 512)
    target_blocks = jnp.arange(top_total, dtype=jnp.int32).reshape(
        top_total // block_rows, block_rows
    )
    top_field = lax.map(
        lambda targets: top_potential(targets, charges_flat, top_z, top_y, top_x, strength),
        target_blocks,
    )
    top_field = top_field.reshape(top_z, top_y, top_x)
    potential = potential + to_fine(
        top_field, top_field.shape, F, plane_ids, line_ids, column_ids, 0, 0
    )
    rimmed_field = extended(potential, (("slab", 0), ("pencil", 1)), 2)
    padded_field = jnp.pad(rimmed_field, ((0, 0), (0, 0), (2, 2)))
    gradients = jnp.stack(
        [gradient_along(padded_field, direction, CZ, CY, NX) for direction in range(3)]
    ).reshape(3, row_cells, NX)

    def pick(block):
        rows_here, columns_here, charges_here = block
        row_table = (rows_here[:, None] == row_range[None, :]).astype(jnp.float32)
        column_table = (columns_here[:, None] == column_range[None, :]).astype(jnp.float32)
        picked_rows = jnp.einsum(
            "ar,drx->adx", row_table, gradients, precision=lax.Precision.HIGHEST
        )
        at_cell = jnp.sum(picked_rows * column_table[:, None, :], axis=2)
        return -charges_here[:, None] * at_cell

    picked = lax.map(pick, (row_blocks, column_blocks, charge_blocks))
    forces = picked.reshape(atom_total, 3).T
    return (potential, forces)


def solution(mesh):
    return jax.shard_map(
        body,
        mesh=mesh,
        in_specs=(P(None, ("slab", "pencil")), P(("slab", "pencil"))),
        out_specs=(P("slab", "pencil", None), P(None, ("slab", "pencil"))),
        check_vma=False,
    )
```

profile of v0, /device:TPU:12, one launch (start us, length us, event | category | flops | bytes accessed | tf_op | source)
XLA Modules:
  0.0 270.0 jit_solution(17136791525805690343)
XLA Ops:
  2.7 18.5 %while.27 = (s32[]{:T(128)}, f32[256,512]{1,0:T(8,128)S(1)}, s32[16,512]{1,0:T(8,128)S(1)}, s32[16,512]{1,0:T(8,128)S(1)}, f32[16,512]{1,0:T(8,128)S(1)}, /*index=5*/s32[]{:T(128)}, s32[]{:T(128)}) while((s32[]{:T(128)}, f32[256,512]{1,0:T(8,128)S(1)}, s32[16,512]{1,0:T(8,128)S(1)}, s32[16,512]{1,0:T(8,128)S(1)}, ...), condition=%wide.region_1.2_spmd.clone, body=%wide.region_0.1_spmd.clone.sunk | while | flops 806223872 | bytes 1067103 | solution.py:152
  21.2 34.9 %reshape_reshape.6 = f32[4,2,16,2,256,2]{5,4,3,2,1,0:T(8,128)} reshape(f32[256,512]{1,0:T(8,128)S(1)} %get-tuple-element.93) | data formatting | bytes 1048576 | tf_op jit(solution)/shard_map/reshape;reshape | solution.py:65
  56.1 11.6 %fusion.1208 = (f32[16,256]{1,0:T(8,128)S(1)}, f32[4,16,256]{2,1,0:T(8,128)S(1)}) fusion(f32[4,2,16,2,256,2]{5,4,3,2,1,0:T(8,128)} %reshape_reshape.6), kind=kLoop, calls=%fused_computation.2077 | loop fusion | flops 241664 | bytes 606208 | tf_op jit(solution)/shard_map/reduce_sum | solution.py:65
  67.7 5.5 %reshape.810 = f32[2,2,8,2,128,2]{5,4,3,2,1,0:T(8,128)} reshape(f32[4,16,256]{2,1,0:T(8,128)S(1)} %get-tuple-element.133) | data formatting | bytes 131072 | tf_op jit(solution)/shard_map/reshape | solution.py:65
  73.2 2.5 reduce_sum.100
  75.7 3.4 %collective-permute-start.12 = (f32[2,8,128]{2,1,0:T(8,128)S(1)}, f32[2,8,128]{2,1,0:T(8,128)S(1)}, u32[]{:S(2)}, u32[]{:S(2)}) collective-permute-start(f32[2,8,128]{2,1,0:T(8,128)S(1)} %reduce_sum.100), channel_id=1, source_target_pairs={{0,4},{4,8},{8,12},{12,16},{16,20},{20,24},{24,28},{1,5},{5,9},{9,... | collective-permute-start | bytes 24584 | tf_op jit(solution)/shard_map/ppermute | solution.py:24
  79.1 3.3 %collective-permute-start.13 = (f32[2,8,128]{2,1,0:T(8,128)S(1)}, f32[2,8,128]{2,1,0:T(8,128)S(1)}, u32[]{:S(2)}, u32[]{:S(2)}) collective-permute-start(f32[2,8,128]{2,1,0:T(8,128)S(1)} %reduce_sum.100), channel_id=1, source_target_pairs={{4,0},{8,4},{12,8},{16,12},{20,16},{24,20},{28,24},{5,1},{9,5},{13... | collective-permute-start | bytes 24584 | tf_op jit(solution)/shard_map/ppermute | solution.py:26
  82.5 2.5 collective-permute-start.4
  85.1 4.2 %collective-permute-start.5 = (f32[2,16,256]{2,0,1:T(2,128)S(1)}, f32[2,16,256]{2,0,1:T(2,128)S(1)}, u32[]{:S(2)}, u32[]{:S(2)}) collective-permute-start(f32[2,16,256]{2,0,1:T(2,128)S(1)} %get-tuple-element.191), channel_id=1, source_target_pairs={{4,0},{8,4},{12,8},{16,12},{20,16},{24,20},{28,24},{5,1},{9,5},{13... | collective-permute-start | bytes 98312 | tf_op jit(solution)/shard_map/ppermute | solution.py:26
  89.3 2.0 collective-permute-start
  95.0 30.5 %all-gather = f32[32,1,336]{2,1,0:T(1,128)S(1)} all-gather(f32[1,1,336]{2,1,0:T(1,128)S(1)} %maximum_bitcast_fusion), channel_id=1, replica_groups=mesh['slab'=8,'pencil'=4] {'slab','pencil'}, dimensions={0}, use_global_device_ids=true | all-gather | bytes 44352 | tf_op jit(solution)/shard_map/all_gather | solution.py:191
  131.1 2.3 collective-permute-start.14
  133.4 4.5 %collective-permute-start.15 = (f32[6,2,128]{2,1,0:T(2,128)S(1)}, f32[6,2,128]{2,1,0:T(2,128)S(1)}, u32[]{:S(2)}, u32[]{:S(2)}) collective-permute-start(f32[6,2,128]{2,1,0:T(2,128)S(1)} %get-tuple-element.195), channel_id=1, source_target_pairs={{1,0},{2,1},{3,2},{5,4},{6,5},{7,6},{9,8},{10,9},{11,10},{13,12},{... | collective-permute-start | bytes 18440 | tf_op jit(solution)/shard_map/ppermute | solution.py:26
  139.6 1.9 collective-permute-start.16
  141.5 6.0 %collective-permute-start.17 = (f32[1,8,128]{2,1,0:T(8,128)S(1)}, f32[1,8,128]{2,1,0:T(8,128)S(1)}, u32[]{:S(2)}, u32[]{:S(2)}) collective-permute-start(f32[1,8,128]{2,1,0:T(8,128)S(1)} %get-tuple-element.199), channel_id=1, source_target_pairs={{4,0},{8,4},{12,8},{16,12},{20,16},{24,20},{28,24},{5,1},{9,5},{13... | collective-permute-start | bytes 12296 | tf_op jit(solution)/shard_map/ppermute | solution.py:26
  147.6 5.4 %collective-permute-start.1 = (f32[2,32,512]{2,1,0:T(8,128)S(1)}, f32[2,32,512]{2,1,0:T(8,128)S(1)}, u32[]{:S(2)}, u32[]{:S(2)}) collective-permute-start(f32[2,32,512]{2,1,0:T(8,128)S(1)} %bitcast.128), channel_id=1, source_target_pairs={{4,0},{8,4},{12,8},{16,12},{20,16},{24,20},{28,24},{5,1},{9,5},{13... | collective-permute-start | bytes 393224 | tf_op jit(solution)/shard_map/ppermute | solution.py:26
  153.1 2.1 collective-permute-start.18
  155.2 3.6 %collective-permute-start.19 = (f32[4,1,128]{2,1,0:T(1,128)S(1)}, f32[4,1,128]{2,1,0:T(1,128)S(1)}, u32[]{:S(2)}, u32[]{:S(2)}) collective-permute-start(f32[4,1,128]{2,1,0:T(1,128)S(1)} %get-tuple-element.197), channel_id=1, source_target_pairs={{1,0},{2,1},{3,2},{5,4},{6,5},{7,6},{9,8},{10,9},{11,10},{13,12},{... | collective-permute-start | bytes 6152 | tf_op jit(solution)/shard_map/ppermute | solution.py:26
  158.9 1.9 collective-permute-start.6
  160.8 3.6 %collective-permute-start.7 = (f32[8,2,256]{2,0,1:T(8,128)S(1)}, f32[8,2,256]{2,0,1:T(8,128)S(1)}, u32[]{:S(2)}, u32[]{:S(2)}) collective-permute-start(f32[8,2,256]{2,0,1:T(8,128)S(1)} %get-tuple-element.185), channel_id=1, source_target_pairs={{1,0},{2,1},{3,2},{5,4},{6,5},{7,6},{9,8},{10,9},{11,10},{13,12},{... | collective-permute-start | bytes 49160 | tf_op jit(solution)/shard_map/ppermute | solution.py:26
  166.2 2.7 %fusion.468 = f32[4,16,256]{2,0,1:T(4,128)S(1)} fusion(f32[8,20,260]{2,0,1:T(8,128)S(1)} %select_maximum_fusion.8, f32[8,18,256]{2,0,1:T(8,128)S(1)} %get-tuple-element.183, f32[2,16,256]{2,0,1:T(2,128)S(1)} %collective-permute-done.5, f32[4,16,256]{2,0,1:T(4,128)S(1)} %copy.47, f32[8,18,256]{2,0,1:T(8,128)S(1)} %get-tuple-element.182, ...), kind=kLoop, calls=%fused_computation.912 | loop fusion | flops 4145152 | bytes 8060928 | tf_op jit(solution)/shard_map/add | solution.py:52
  170.9 4.8 %collective-permute-start.9 = (f32[1,16,256]{2,0,1:T(1,128)S(1)}, f32[1,16,256]{2,0,1:T(1,128)S(1)}, u32[]{:S(2)}, u32[]{:S(2)}) collective-permute-start(f32[1,16,256]{2,0,1:T(1,128)S(1)} %get-tuple-element.189), channel_id=1, source_target_pairs={{4,0},{8,4},{12,8},{16,12},{20,16},{24,20},{28,24},{5,1},{9,5},{13... | collective-permute-start | bytes 49160 | tf_op jit(solution)/shard_map/ppermute | solution.py:26
  177.2 1.9 collective-permute-start.10
  179.1 3.6 %collective-permute-start.11 = (f32[6,1,256]{2,0,1:T(8,128)S(1)}, f32[6,1,256]{2,0,1:T(8,128)S(1)}, u32[]{:S(2)}, u32[]{:S(2)}) collective-permute-start(f32[6,1,256]{2,0,1:T(8,128)S(1)} %get-tuple-element.187), channel_id=1, source_target_pairs={{1,0},{2,1},{3,2},{5,4},{6,5},{7,6},{9,8},{10,9},{11,10},{13,12},{... | collective-permute-start | bytes 18440 | tf_op jit(solution)/shard_map/ppermute | solution.py:26
  184.5 1.9 collective-permute-start.2
  186.4 3.6 %collective-permute-start.3 = (f32[12,2,512]{2,1,0:T(2,128)S(1)}, f32[12,2,512]{2,1,0:T(2,128)S(1)}, u32[]{:S(2)}, u32[]{:S(2)}) collective-permute-start(f32[12,2,512]{2,1,0:T(2,128)S(1)} %get-tuple-element.177), channel_id=1, source_target_pairs={{1,0},{2,1},{3,2},{5,4},{6,5},{7,6},{9,8},{10,9},{11,10},{13,12},{... | collective-permute-start | bytes 147464 | tf_op jit(solution)/shard_map/ppermute | solution.py:26
  192.5 10.7 %convolution_add_fusion.5 = f32[8,32,512]{2,1,0:T(8,128)S(1)} fusion(f32[8,32,256]{2,1,0:T(8,128)S(1)} %convolution_bitcast_fusion, f32[12,36,516]{2,1,0:T(8,128)S(1)} %select_maximum_fusion.4, f32[12,34,512]{2,1,0:T(8,128)S(1)} %get-tuple-element.175, f32[2,32,512]{2,1,0:T(8,128)S(1)} %collective-permute-done.1, f32[8,32,512]{2,1,0:T(8,128)S(1)} %bitcast.118, ...), kind=kOutput, calls=%fused_computation.282 | convolution fusion | flops 436600832 | bytes 64495616 | tf_op jit(solution)/shard_map/fc,abc->abf/dot_general | solution.py:91
  206.7 5.1 %collective-permute-start.20 = (f32[2,32,512]{2,1,0:T(8,128)S(1)}, f32[2,32,512]{2,1,0:T(8,128)S(1)}, u32[]{:S(2)}, u32[]{:S(2)}) collective-permute-start(f32[2,32,512]{2,1,0:T(8,128)S(1)} %get-tuple-element.179), channel_id=1, source_target_pairs={{4,0},{8,4},{12,8},{16,12},{20,16},{24,20},{28,24},{5,1},{9,5},{13... | collective-permute-start | bytes 393224 | tf_op jit(solution)/shard_map/ppermute | solution.py:26
  214.3 5.3 %collective-permute-done.21 = f32[2,32,512]{2,1,0:T(8,128)S(1)} collective-permute-done((f32[2,32,512]{2,1,0:T(8,128)S(1)}, f32[2,32,512]{2,1,0:T(8,128)S(1)}, u32[]{:S(2)}, u32[]{:S(2)}) %collective-permute-start.21) | collective-permute-done | bytes 131104 | tf_op jit(solution)/shard_map/ppermute | solution.py:24
  219.6 2.6 collective-permute-start.22
  224.5 3.1 %collective-permute-done.23 = f32[12,2,512]{2,1,0:T(2,128)S(1)} collective-permute-done((f32[12,2,512]{2,1,0:T(2,128)S(1)}, f32[12,2,512]{2,1,0:T(2,128)S(1)}, u32[]{:S(2)}, u32[]{:S(2)}) %collective-permute-start.23) | collective-permute-done | bytes 49184 | tf_op jit(solution)/shard_map/ppermute | solution.py:24
  229.6 40.4 %while.26 = (s32[]{:T(128)}, f32[16,512,3]{1,2,0:T(4,128)}, f32[16,512]{1,0:T(8,128)S(1)}, s32[16,512]{1,0:T(8,128)S(1)}, f32[3,256,512]{1,2,0:T(8,128)S(1)}, /*index=5*/s32[16,512]{1,0:T(8,128)S(1)}, s32[]{:T(128)}) while((s32[]{:T(128)}, f32[16,512,3]{1,2,0:T(4,128)}, f32[16,512]{1,0:T(8,128)S(1)}, s32[16,512]{1,0:T(8,128)S(1)}, ...), condition=%wide.region_18.19_spmd.clone, body=%wide.region_16.18_spmd.clone.sunk | while | flops 2418147840 | bytes 3709525 | solution.py:251
  (270 shorter events, 89.9 us)
Async XLA Ops:
  75.7 55.4 %collective-permute-start.12 = (f32[2,8,128]{2,1,0:T(8,128)S(1)}, f32[2,8,128]{2,1,0:T(8,128)S(1)}, u32[]{:S(2)}, u32[]{:S(2)}) collective-permute-start(f32[2,8,128]{2,1,0:T(8,128)S(1)} %reduce_sum.100), channel_id=1, source_target_pairs={{0,4},{4,8},{8,12},{12,16},{16,20},{20,24},{24,28},{1,5},{5,9},{9,... | collective-permute-start | bytes 24584 | tf_op jit(solution)/shard_map/ppermute | solution.py:24
  79.1 52.0 %collective-permute-start.13 = (f32[2,8,128]{2,1,0:T(8,128)S(1)}, f32[2,8,128]{2,1,0:T(8,128)S(1)}, u32[]{:S(2)}, u32[]{:S(2)}) collective-permute-start(f32[2,8,128]{2,1,0:T(8,128)S(1)} %reduce_sum.100), channel_id=1, source_target_pairs={{4,0},{8,4},{12,8},{16,12},{20,16},{24,20},{28,24},{5,1},{9,5},{13... | collective-permute-start | bytes 24584 | tf_op jit(solution)/shard_map/ppermute | solution.py:26
  82.5 72.6 %collective-permute-start.4 = (f32[2,16,256]{2,0,1:T(2,128)S(1)}, f32[2,16,256]{2,0,1:T(2,128)S(1)}, u32[]{:S(2)}, u32[]{:S(2)}) collective-permute-start(f32[2,16,256]{2,0,1:T(2,128)S(1)} %get-tuple-element.190), channel_id=1, source_target_pairs={{0,4},{4,8},{8,12},{12,16},{16,20},{20,24},{24,28},{1,5},{5,9},{9,... | collective-permute-start | bytes 98312 | tf_op jit(solution)/shard_map/ppermute | solution.py:24
  85.1 73.8 %collective-permute-start.5 = (f32[2,16,256]{2,0,1:T(2,128)S(1)}, f32[2,16,256]{2,0,1:T(2,128)S(1)}, u32[]{:S(2)}, u32[]{:S(2)}) collective-permute-start(f32[2,16,256]{2,0,1:T(2,128)S(1)} %get-tuple-element.191), channel_id=1, source_target_pairs={{4,0},{8,4},{12,8},{16,12},{20,16},{24,20},{28,24},{5,1},{9,5},{13... | collective-permute-start | bytes 98312 | tf_op jit(solution)/shard_map/ppermute | solution.py:26
  89.3 95.1 %collective-permute-start = (f32[2,32,512]{2,1,0:T(8,128)S(1)}, f32[2,32,512]{2,1,0:T(8,128)S(1)}, u32[]{:S(2)}, u32[]{:S(2)}) collective-permute-start(f32[2,32,512]{2,1,0:T(8,128)S(1)} %bitcast.129), channel_id=1, source_target_pairs={{0,4},{4,8},{8,12},{12,16},{16,20},{20,24},{24,28},{1,5},{5,9},{9,... | collective-permute-start | bytes 393224 | tf_op jit(solution)/shard_map/ppermute | solution.py:24
  131.1 6.8 %collective-permute-start.14 = (f32[6,2,128]{2,1,0:T(2,128)S(1)}, f32[6,2,128]{2,1,0:T(2,128)S(1)}, u32[]{:S(2)}, u32[]{:S(2)}) collective-permute-start(f32[6,2,128]{2,1,0:T(2,128)S(1)} %get-tuple-element.194), channel_id=1, source_target_pairs={{0,1},{1,2},{2,3},{4,5},{5,6},{6,7},{8,9},{9,10},{10,11},{12,13},{... | collective-permute-start | bytes 18440 | tf_op jit(solution)/shard_map/ppermute | solution.py:24
  133.4 5.8 %collective-permute-start.15 = (f32[6,2,128]{2,1,0:T(2,128)S(1)}, f32[6,2,128]{2,1,0:T(2,128)S(1)}, u32[]{:S(2)}, u32[]{:S(2)}) collective-permute-start(f32[6,2,128]{2,1,0:T(2,128)S(1)} %get-tuple-element.195), channel_id=1, source_target_pairs={{1,0},{2,1},{3,2},{5,4},{6,5},{7,6},{9,8},{10,9},{11,10},{13,12},{... | collective-permute-start | bytes 18440 | tf_op jit(solution)/shard_map/ppermute | solution.py:26
  139.6 8.0 %collective-permute-start.16 = (f32[1,8,128]{2,1,0:T(8,128)S(1)}, f32[1,8,128]{2,1,0:T(8,128)S(1)}, u32[]{:S(2)}, u32[]{:S(2)}) collective-permute-start(f32[1,8,128]{2,1,0:T(8,128)S(1)} %get-tuple-element.198), channel_id=1, source_target_pairs={{0,4},{4,8},{8,12},{12,16},{16,20},{20,24},{24,28},{1,5},{5,9},{9,... | collective-permute-start | bytes 12296 | tf_op jit(solution)/shard_map/ppermute | solution.py:24
  141.5 11.5 %collective-permute-start.17 = (f32[1,8,128]{2,1,0:T(8,128)S(1)}, f32[1,8,128]{2,1,0:T(8,128)S(1)}, u32[]{:S(2)}, u32[]{:S(2)}) collective-permute-start(f32[1,8,128]{2,1,0:T(8,128)S(1)} %get-tuple-element.199), channel_id=1, source_target_pairs={{4,0},{8,4},{12,8},{16,12},{20,16},{24,20},{28,24},{5,1},{9,5},{13... | collective-permute-start | bytes 12296 | tf_op jit(solution)/shard_map/ppermute | solution.py:26
  147.6 36.8 %collective-permute-start.1 = (f32[2,32,512]{2,1,0:T(8,128)S(1)}, f32[2,32,512]{2,1,0:T(8,128)S(1)}, u32[]{:S(2)}, u32[]{:S(2)}) collective-permute-start(f32[2,32,512]{2,1,0:T(8,128)S(1)} %bitcast.128), channel_id=1, source_target_pairs={{4,0},{8,4},{12,8},{16,12},{20,16},{24,20},{28,24},{5,1},{9,5},{13... | collective-permute-start | bytes 393224 | tf_op jit(solution)/shard_map/ppermute | solution.py:26
  153.1 7.7 %collective-permute-start.18 = (f32[4,1,128]{2,1,0:T(1,128)S(1)}, f32[4,1,128]{2,1,0:T(1,128)S(1)}, u32[]{:S(2)}, u32[]{:S(2)}) collective-permute-start(f32[4,1,128]{2,1,0:T(1,128)S(1)} %get-tuple-element.196), channel_id=1, source_target_pairs={{0,1},{1,2},{2,3},{4,5},{5,6},{6,7},{8,9},{9,10},{10,11},{12,13},{... | collective-permute-start | bytes 6152 | tf_op jit(solution)/shard_map/ppermute | solution.py:24
  155.2 9.3 %collective-permute-start.19 = (f32[4,1,128]{2,1,0:T(1,128)S(1)}, f32[4,1,128]{2,1,0:T(1,128)S(1)}, u32[]{:S(2)}, u32[]{:S(2)}) collective-permute-start(f32[4,1,128]{2,1,0:T(1,128)S(1)} %get-tuple-element.197), channel_id=1, source_target_pairs={{1,0},{2,1},{3,2},{5,4},{6,5},{7,6},{9,8},{10,9},{11,10},{13,12},{... | collective-permute-start | bytes 6152 | tf_op jit(solution)/shard_map/ppermute | solution.py:26
  158.9 5.6 %collective-permute-start.6 = (f32[8,2,256]{2,0,1:T(8,128)S(1)}, f32[8,2,256]{2,0,1:T(8,128)S(1)}, u32[]{:S(2)}, u32[]{:S(2)}) collective-permute-start(f32[8,2,256]{2,0,1:T(8,128)S(1)} %get-tuple-element.184), channel_id=1, source_target_pairs={{0,1},{1,2},{2,3},{4,5},{5,6},{6,7},{8,9},{9,10},{10,11},{12,13},{... | collective-permute-start | bytes 49160 | tf_op jit(solution)/shard_map/ppermute | solution.py:24
  160.8 5.1 %collective-permute-start.7 = (f32[8,2,256]{2,0,1:T(8,128)S(1)}, f32[8,2,256]{2,0,1:T(8,128)S(1)}, u32[]{:S(2)}, u32[]{:S(2)}) collective-permute-start(f32[8,2,256]{2,0,1:T(8,128)S(1)} %get-tuple-element.185), channel_id=1, source_target_pairs={{1,0},{2,1},{3,2},{5,4},{6,5},{7,6},{9,8},{10,9},{11,10},{13,12},{... | collective-permute-start | bytes 49160 | tf_op jit(solution)/shard_map/ppermute | solution.py:26
  169.0 7.0 %collective-permute-start.8 = (f32[1,16,256]{2,0,1:T(1,128)S(1)}, f32[1,16,256]{2,0,1:T(1,128)S(1)}, u32[]{:S(2)}, u32[]{:S(2)}) collective-permute-start(f32[1,16,256]{2,0,1:T(1,128)S(1)} %get-tuple-element.188), channel_id=1, source_target_pairs={{0,4},{4,8},{8,12},{12,16},{16,20},{20,24},{24,28},{1,5},{5,9},{9,... | collective-permute-start | bytes 49160 | tf_op jit(solution)/shard_map/ppermute | solution.py:24
  170.9 6.3 %collective-permute-start.9 = (f32[1,16,256]{2,0,1:T(1,128)S(1)}, f32[1,16,256]{2,0,1:T(1,128)S(1)}, u32[]{:S(2)}, u32[]{:S(2)}) collective-permute-start(f32[1,16,256]{2,0,1:T(1,128)S(1)} %get-tuple-element.189), channel_id=1, source_target_pairs={{4,0},{8,4},{12,8},{16,12},{20,16},{24,20},{28,24},{5,1},{9,5},{13... | collective-permute-start | bytes 49160 | tf_op jit(solution)/shard_map/ppermute | solution.py:26
  177.2 5.9 %collective-permute-start.10 = (f32[6,1,256]{2,0,1:T(8,128)S(1)}, f32[6,1,256]{2,0,1:T(8,128)S(1)}, u32[]{:S(2)}, u32[]{:S(2)}) collective-permute-start(f32[6,1,256]{2,0,1:T(8,128)S(1)} %get-tuple-element.186), channel_id=1, source_target_pairs={{0,1},{1,2},{2,3},{4,5},{5,6},{6,7},{8,9},{9,10},{10,11},{12,13},{... | collective-permute-start | bytes 18440 | tf_op jit(solution)/shard_map/ppermute | solution.py:24
  179.1 5.0 %collective-permute-start.11 = (f32[6,1,256]{2,0,1:T(8,128)S(1)}, f32[6,1,256]{2,0,1:T(8,128)S(1)}, u32[]{:S(2)}, u32[]{:S(2)}) collective-permute-start(f32[6,1,256]{2,0,1:T(8,128)S(1)} %get-tuple-element.187), channel_id=1, source_target_pairs={{1,0},{2,1},{3,2},{5,4},{6,5},{7,6},{9,8},{10,9},{11,10},{13,12},{... | collective-permute-start | bytes 18440 | tf_op jit(solution)/shard_map/ppermute | solution.py:26
  184.5 6.0 %collective-permute-start.2 = (f32[12,2,512]{2,1,0:T(2,128)S(1)}, f32[12,2,512]{2,1,0:T(2,128)S(1)}, u32[]{:S(2)}, u32[]{:S(2)}) collective-permute-start(f32[12,2,512]{2,1,0:T(2,128)S(1)} %get-tuple-element.176), channel_id=1, source_target_pairs={{0,1},{1,2},{2,3},{4,5},{5,6},{6,7},{8,9},{9,10},{10,11},{12,13},{... | collective-permute-start | bytes 147464 | tf_op jit(solution)/shard_map/ppermute | solution.py:24
  186.4 5.4 %collective-permute-start.3 = (f32[12,2,512]{2,1,0:T(2,128)S(1)}, f32[12,2,512]{2,1,0:T(2,128)S(1)}, u32[]{:S(2)}, u32[]{:S(2)}) collective-permute-start(f32[12,2,512]{2,1,0:T(2,128)S(1)} %get-tuple-element.177), channel_id=1, source_target_pairs={{1,0},{2,1},{3,2},{5,4},{6,5},{7,6},{9,8},{10,9},{11,10},{13,12},{... | collective-permute-start | bytes 147464 | tf_op jit(solution)/shard_map/ppermute | solution.py:26
  206.7 21.6 %copy-start = (f32[8,32,512]{2,1,0:T(8,128)}, f32[8,32,512]{2,1,0:T(8,128)S(1)}, u32[]{:S(2)}) copy-start(f32[8,32,512]{2,1,0:T(8,128)S(1)} %convolution_add_fusion.1) | copy-start | bytes 1572868
  206.7 7.6 %collective-permute-start.20 = (f32[2,32,512]{2,1,0:T(8,128)S(1)}, f32[2,32,512]{2,1,0:T(8,128)S(1)}, u32[]{:S(2)}, u32[]{:S(2)}) collective-permute-start(f32[2,32,512]{2,1,0:T(8,128)S(1)} %get-tuple-element.179), channel_id=1, source_target_pairs={{4,0},{8,4},{12,8},{16,12},{20,16},{24,20},{28,24},{5,1},{9,5},{13... | collective-permute-start | bytes 393224 | tf_op jit(solution)/shard_map/ppermute | solution.py:26
  211.8 7.8 %collective-permute-start.21 = (f32[2,32,512]{2,1,0:T(8,128)S(1)}, f32[2,32,512]{2,1,0:T(8,128)S(1)}, u32[]{:S(2)}, u32[]{:S(2)}) collective-permute-start(f32[2,32,512]{2,1,0:T(8,128)S(1)} %get-tuple-element.178), channel_id=1, source_target_pairs={{0,4},{4,8},{8,12},{12,16},{16,20},{20,24},{24,28},{1,5},{5,9},{9,... | collective-permute-start | bytes 393224 | tf_op jit(solution)/shard_map/ppermute | solution.py:24
  219.6 4.8 %collective-permute-start.22 = (f32[12,2,512]{2,1,0:T(2,128)S(1)}, f32[12,2,512]{2,1,0:T(2,128)S(1)}, u32[]{:S(2)}, u32[]{:S(2)}) collective-permute-start(f32[12,2,512]{2,1,0:T(2,128)S(1)} %get-tuple-element.173), channel_id=1, source_target_pairs={{1,0},{2,1},{3,2},{5,4},{6,5},{7,6},{9,8},{10,9},{11,10},{13,12},{... | collective-permute-start | bytes 147464 | tf_op jit(solution)/shard_map/ppermute | solution.py:26
  222.2 5.4 %collective-permute-start.23 = (f32[12,2,512]{2,1,0:T(2,128)S(1)}, f32[12,2,512]{2,1,0:T(2,128)S(1)}, u32[]{:S(2)}, u32[]{:S(2)}) collective-permute-start(f32[12,2,512]{2,1,0:T(2,128)S(1)} %get-tuple-element.172), channel_id=1, source_target_pairs={{0,1},{1,2},{2,3},{4,5},{5,6},{6,7},{8,9},{9,10},{10,11},{12,13},{... | collective-permute-start | bytes 147464 | tf_op jit(solution)/shard_map/ppermute | solution.py:24
where the time goes:
time: 271 us; the launch traced here: 270 us
  starting transfers between devices  76.4 us (28%)
  matrix products  65.5 us (24%)
  local copies, waits for them, and re-layouts  44.9 us (17%)
  other arithmetic  35 us (13%)
  blocking collectives  30.5 us (11%)
  waiting for transfers between devices  15.1 us (6%)
    ppermute x12, starting transfers between devices, extended(): lax.ppermute(head, axis, [((i + 1) % count, i) for i in range(ends)])  50.6 us
    another operation x1, local copies, waits for them, and re-layouts, restrict(): grid.reshape(planes // 2, 2, rows // 2, 2, length // 2, 2)  34.9 us
    all_gather x1, blocking collectives, body(): gathered = lax.all_gather(packed, ('slab', 'pencil'), axis=0, tiled=True)  30.5 us
    dot_general x16, matrix products, pick(): jnp.einsum('ar,drx->adx', row_table, gradients, precision=lax.Precision.H...  27.9 us
    ppermute x12, starting transfers between devices, extended(): lax.ppermute(tail, axis, [(i, (i + 1) % count) for i in range(ends)])  25.7 us
    dot_general x16, matrix products, deposit(): added = jnp.dot(row_table.T, column_table, precision=lax.Precision.HIGHEST)  17.4 us
    reduce_sum x4, other arithmetic, restrict(): grid.reshape(planes // 2, 2, rows // 2, 2, length // 2, 2)  14.4 us
    dot_general x5, matrix products, to_fine(): jnp.einsum('fc,abc->abf', along_x, section, precision=lax.Precision.HIGHEST)  14.1 us
  transfers between devices with their start and end apart: 24, of which 8 were waited for; matrix products, arithmetic and copies ran while one was open for 5% of the time, Pallas kernels for 0%

commit v1 on v0

--- a/solution.py
+++ b/solution.py
@@ -188,7 +188,12 @@
         partial_plane = restrict_plane(partial_plane)
         pieces.append(partial_plane)
     packed = jnp.concatenate([piece.reshape(1, -1) for piece in pieces], axis=1)
-    gathered = lax.all_gather(packed, ("slab", "pencil"), axis=0, tiled=True)
+    gathered = jnp.concatenate(
+        lax.all_to_all(
+            jnp.stack([packed] * lax.axis_size(("slab", "pencil"))), ("slab", "pencil"), 0, 0
+        ),
+        axis=0,
+    )
     coarse = []
     offset = 0
     for step, piece in enumerate(pieces):

time: 271 us -> 242 us (0.89)
  blocking collectives: 30.5 us -> 0 us
    all_gather x1 -> x0, blocking collectives: 30.5 us -> none  [body(): gathered = lax.all_gather(packed, ('slab', 'pencil'), axis=0, tiled=True)]
    ppermute x12, starting transfers between devices: 50.6 us -> 40.8 us  [extended(): lax.ppermute(head, axis, [((i + 1) % count, i) for i in range(ends)])]
    all_to_all x0 -> x1, starting transfers between devices: none -> 6.4 us  [body(): lax.all_to_all(jnp.stack([packed] * lax.axis_size(('slab', 'pencil'))), (...]
    ppermute x12, starting transfers between devices: 25.7 us -> 29 us  [extended(): lax.ppermute(tail, axis, [(i, (i + 1) % count) for i in range(ends)])]
    ppermute x12, waiting for transfers between devices: 6.72 us -> 9.87 us  [extended(): lax.ppermute(head, axis, [((i + 1) % count, i) for i in range(ends)])]
  transfers between devices with their start and end apart: 24 -> 25, of which waited for: 8 -> 8; matrix products, arithmetic and copies ran while one was open for 5% -> 6% of each run, Pallas kernels for 0% -> 0%
where the time goes in v1:
time: 242 us; the launch traced here: 241 us
  starting transfers between devices  76.2 us (31%)
  matrix products  63.2 us (26%)
  local copies, waits for them, and re-layouts  45.5 us (19%)
  other arithmetic  36.9 us (15%)
  waiting for transfers between devices  16.3 us (7%)
    ppermute x12, starting transfers between devices, extended(): lax.ppermute(head, axis, [((i + 1) % count, i) for i in range(ends)])  40.8 us
    another operation x1, local copies, waits for them, and re-layouts, restrict(): grid.reshape(planes // 2, 2, rows // 2, 2, length // 2, 2)  34.9 us
    ppermute x12, starting transfers between devices, extended(): lax.ppermute(tail, axis, [(i, (i + 1) % count) for i in range(ends)])  29 us
    dot_general x16, matrix products, pick(): jnp.einsum('ar,drx->adx', row_table, gradients, precision=lax.Precision.H...  27.9 us
    dot_general x16, matrix products, deposit(): added = jnp.dot(row_table.T, column_table, precision=lax.Precision.HIGHEST)  17.4 us
    reduce_sum x4, other arithmetic, restrict(): grid.reshape(planes // 2, 2, rows // 2, 2, length // 2, 2)  14.4 us
    dot_general x5, matrix products, to_fine(): jnp.einsum('fc,abc->abf', along_x, section, precision=lax.Precision.HIGHEST)  14.1 us
    ppermute x12, waiting for transfers between devices, extended(): lax.ppermute(head, axis, [((i + 1) % count, i) for i in range(ends)])  9.87 us
  transfers between devices with their start and end apart: 25, of which 8 were waited for; matrix products, arithmetic and copies ran while one was open for 6% of the time, Pallas kernels for 0%

profile of v1, /device:TPU:12, one launch (start us, length us, event | category | flops | bytes accessed | tf_op | source)
XLA Modules:
  0.0 240.7 jit_solution(6588911675702108927)
XLA Ops:
  2.7 18.5 %while.27 = (s32[]{:T(128)}, f32[256,512]{1,0:T(8,128)S(1)}, s32[16,512]{1,0:T(8,128)S(1)}, s32[16,512]{1,0:T(8,128)S(1)}, f32[16,512]{1,0:T(8,128)S(1)}, /*index=5*/s32[]{:T(128)}, s32[]{:T(128)}) while((s32[]{:T(128)}, f32[256,512]{1,0:T(8,128)S(1)}, s32[16,512]{1,0:T(8,128)S(1)}, s32[16,512]{1,0:T(8,128)S(1)}, ...), condition=%wide.region_1.2_spmd.clone, body=%wide.region_0.1_spmd.clone.sunk | while | flops 806223872 | bytes 1067103 | solution.py:152
  21.2 34.9 %reshape_reshape.6 = f32[4,2,16,2,256,2]{5,4,3,2,1,0:T(8,128)} reshape(f32[256,512]{1,0:T(8,128)S(1)} %get-tuple-element.93) | data formatting | bytes 1048576 | tf_op jit(solution)/shard_map/reshape;reshape | solution.py:65
  56.1 11.6 %fusion.1154 = (f32[16,256]{1,0:T(8,128)S(1)}, f32[4,16,256]{2,1,0:T(8,128)S(1)}) fusion(f32[4,2,16,2,256,2]{5,4,3,2,1,0:T(8,128)} %reshape_reshape.6), kind=kLoop, calls=%fused_computation.2039 | loop fusion | flops 241664 | bytes 606208 | tf_op jit(solution)/shard_map/reduce_sum | solution.py:65
  67.7 5.5 %reshape.816 = f32[2,2,8,2,128,2]{5,4,3,2,1,0:T(8,128)} reshape(f32[4,16,256]{2,1,0:T(8,128)S(1)} %get-tuple-element.133) | data formatting | bytes 131072 | tf_op jit(solution)/shard_map/reshape | solution.py:65
  73.2 2.5 %reduce_sum.100 = f32[2,8,128]{2,1,0:T(8,128)S(1)} reduce(f32[2,2,8,2,128,2]{5,4,3,2,1,0:T(8,128)} %reshape.816, f32[]{:T(128)} %constant.447.clone.1), dimensions={1,3,5}, to_apply=%region_3.4 | reduce | flops 14336 | bytes 73732 | tf_op jit(solution)/shard_map/reduce_sum | solution.py:65
  75.7 3.4 %collective-permute-start.12 = (f32[2,8,128]{2,1,0:T(8,128)S(1)}, f32[2,8,128]{2,1,0:T(8,128)S(1)}, u32[]{:S(2)}, u32[]{:S(2)}) collective-permute-start(f32[2,8,128]{2,1,0:T(8,128)S(1)} %reduce_sum.100), channel_id=1, source_target_pairs={{0,4},{4,8},{8,12},{12,16},{16,20},{20,24},{24,28},{1,5},{5,9},{9,... | collective-permute-start | bytes 24584 | tf_op jit(solution)/shard_map/ppermute | solution.py:24
  79.1 3.3 %collective-permute-start.13 = (f32[2,8,128]{2,1,0:T(8,128)S(1)}, f32[2,8,128]{2,1,0:T(8,128)S(1)}, u32[]{:S(2)}, u32[]{:S(2)}) collective-permute-start(f32[2,8,128]{2,1,0:T(8,128)S(1)} %reduce_sum.100), channel_id=1, source_target_pairs={{4,0},{8,4},{12,8},{16,12},{20,16},{24,20},{28,24},{5,1},{9,5},{13... | collective-permute-start | bytes 24584 | tf_op jit(solution)/shard_map/ppermute | solution.py:26
  82.6 2.5 %collective-permute-start.4 = (f32[2,16,256]{2,0,1:T(2,128)S(1)}, f32[2,16,256]{2,0,1:T(2,128)S(1)}, u32[]{:S(2)}, u32[]{:S(2)}) collective-permute-start(f32[2,16,256]{2,0,1:T(2,128)S(1)} %get-tuple-element.190), channel_id=1, source_target_pairs={{0,4},{4,8},{8,12},{12,16},{16,20},{20,24},{24,28},{1,5},{5,9},{9,... | collective-permute-start | bytes 98312 | tf_op jit(solution)/shard_map/ppermute | solution.py:24
  85.1 4.2 %collective-permute-start.5 = (f32[2,16,256]{2,0,1:T(2,128)S(1)}, f32[2,16,256]{2,0,1:T(2,128)S(1)}, u32[]{:S(2)}, u32[]{:S(2)}) collective-permute-start(f32[2,16,256]{2,0,1:T(2,128)S(1)} %get-tuple-element.191), channel_id=1, source_target_pairs={{4,0},{8,4},{12,8},{16,12},{20,16},{24,20},{28,24},{5,1},{9,5},{13... | collective-permute-start | bytes 98312 | tf_op jit(solution)/shard_map/ppermute | solution.py:26
  89.3 2.0 collective-permute-start
  95.4 6.4 %all-to-all-start = ((f32[32,1,336]{2,1,0:T(1,128)}), f32[32,1,336]{2,1,0:T(1,128)S(1)}, u32[]{:S(2)}, u32[]{:S(2)}) async-start(f32[32,1,336]{2,1,0:T(1,128)} %stack.10), calls=%async_computation | async-start | bytes 98304 | tf_op jit(solution)/shard_map/all_to_all | solution.py:192
  102.5 2.0 collective-permute-start.14
  104.5 3.5 %collective-permute-start.15 = (f32[6,2,128]{2,1,0:T(2,128)S(1)}, f32[6,2,128]{2,1,0:T(2,128)S(1)}, u32[]{:S(2)}, u32[]{:S(2)}) collective-permute-start(f32[6,2,128]{2,1,0:T(2,128)S(1)} %get-tuple-element.195), channel_id=1, source_target_pairs={{1,0},{2,1},{3,2},{5,4},{6,5},{7,6},{9,8},{10,9},{11,10},{13,12},{... | collective-permute-start | bytes 18440 | tf_op jit(solution)/shard_map/ppermute | solution.py:26
  109.8 3.4 %collective-permute-start.16 = (f32[1,8,128]{2,1,0:T(8,128)S(1)}, f32[1,8,128]{2,1,0:T(8,128)S(1)}, u32[]{:S(2)}, u32[]{:S(2)}) collective-permute-start(f32[1,8,128]{2,1,0:T(8,128)S(1)} %get-tuple-element.198), channel_id=1, source_target_pairs={{0,4},{4,8},{8,12},{12,16},{16,20},{20,24},{24,28},{1,5},{5,9},{9,... | collective-permute-start | bytes 12296 | tf_op jit(solution)/shard_map/ppermute | solution.py:24
  113.2 3.4 %collective-permute-start.17 = (f32[1,8,128]{2,1,0:T(8,128)S(1)}, f32[1,8,128]{2,1,0:T(8,128)S(1)}, u32[]{:S(2)}, u32[]{:S(2)}) collective-permute-start(f32[1,8,128]{2,1,0:T(8,128)S(1)} %get-tuple-element.199), channel_id=1, source_target_pairs={{4,0},{8,4},{12,8},{16,12},{20,16},{24,20},{28,24},{5,1},{9,5},{13... | collective-permute-start | bytes 12296 | tf_op jit(solution)/shard_map/ppermute | solution.py:26
  116.6 2.5 %collective-permute-start.1 = (f32[2,32,512]{2,1,0:T(8,128)S(1)}, f32[2,32,512]{2,1,0:T(8,128)S(1)}, u32[]{:S(2)}, u32[]{:S(2)}) collective-permute-start(f32[2,32,512]{2,1,0:T(8,128)S(1)} %bitcast.126), channel_id=1, source_target_pairs={{4,0},{8,4},{12,8},{16,12},{20,16},{24,20},{28,24},{5,1},{9,5},{13... | collective-permute-start | bytes 393224 | tf_op jit(solution)/shard_map/ppermute | solution.py:26
  121.0 3.6 %collective-permute-start.19 = (f32[4,1,128]{2,1,0:T(1,128)S(1)}, f32[4,1,128]{2,1,0:T(1,128)S(1)}, u32[]{:S(2)}, u32[]{:S(2)}) collective-permute-start(f32[4,1,128]{2,1,0:T(1,128)S(1)} %get-tuple-element.197), channel_id=1, source_target_pairs={{1,0},{2,1},{3,2},{5,4},{6,5},{7,6},{9,8},{10,9},{11,10},{13,12},{... | collective-permute-start | bytes 6152 | tf_op jit(solution)/shard_map/ppermute | solution.py:26
  126.6 3.6 %collective-permute-start.7 = (f32[8,2,256]{2,0,1:T(8,128)S(1)}, f32[8,2,256]{2,0,1:T(8,128)S(1)}, u32[]{:S(2)}, u32[]{:S(2)}) collective-permute-start(f32[8,2,256]{2,0,1:T(8,128)S(1)} %get-tuple-element.185), channel_id=1, source_target_pairs={{1,0},{2,1},{3,2},{5,4},{6,5},{7,6},{9,8},{10,9},{11,10},{13,12},{... | collective-permute-start | bytes 49160 | tf_op jit(solution)/shard_map/ppermute | solution.py:26
  132.0 2.7 %fusion.468 = f32[4,16,256]{2,0,1:T(4,128)S(1)} fusion(f32[8,20,260]{2,0,1:T(8,128)S(1)} %select_maximum_fusion.8, f32[8,18,256]{2,0,1:T(8,128)S(1)} %get-tuple-element.183, f32[2,16,256]{2,0,1:T(2,128)S(1)} %collective-permute-done.5, f32[4,16,256]{2,0,1:T(4,128)S(1)} %copy.59, f32[8,18,256]{2,0,1:T(8,128)S(1)} %get-tuple-element.182, ...), kind=kLoop, calls=%fused_computation.912 | loop fusion | flops 4145152 | bytes 8060928 | tf_op jit(solution)/shard_map/add | solution.py:52
  134.8 3.9 %collective-permute-start.8 = (f32[1,16,256]{2,0,1:T(1,128)S(1)}, f32[1,16,256]{2,0,1:T(1,128)S(1)}, u32[]{:S(2)}, u32[]{:S(2)}) collective-permute-start(f32[1,16,256]{2,0,1:T(1,128)S(1)} %get-tuple-element.188), channel_id=1, source_target_pairs={{0,4},{4,8},{8,12},{12,16},{16,20},{20,24},{24,28},{1,5},{5,9},{9,... | collective-permute-start | bytes 49160 | tf_op jit(solution)/shard_map/ppermute | solution.py:24
  138.7 2.8 %collective-permute-start.9 = (f32[1,16,256]{2,0,1:T(1,128)S(1)}, f32[1,16,256]{2,0,1:T(1,128)S(1)}, u32[]{:S(2)}, u32[]{:S(2)}) collective-permute-start(f32[1,16,256]{2,0,1:T(1,128)S(1)} %get-tuple-element.189), channel_id=1, source_target_pairs={{4,0},{8,4},{12,8},{16,12},{20,16},{24,20},{28,24},{5,1},{9,5},{13... | collective-permute-start | bytes 49160 | tf_op jit(solution)/shard_map/ppermute | solution.py:26
  141.8 2.5 %collective-permute-done.9 = f32[1,16,256]{2,0,1:T(1,128)S(1)} collective-permute-done((f32[1,16,256]{2,0,1:T(1,128)S(1)}, f32[1,16,256]{2,0,1:T(1,128)S(1)}, u32[]{:S(2)}, u32[]{:S(2)}) %collective-permute-start.9) | collective-permute-done | bytes 16416 | tf_op jit(solution)/shard_map/ppermute | solution.py:26
  146.3 3.8 %collective-permute-start.11 = (f32[6,1,256]{2,0,1:T(8,128)S(1)}, f32[6,1,256]{2,0,1:T(8,128)S(1)}, u32[]{:S(2)}, u32[]{:S(2)}) collective-permute-start(f32[6,1,256]{2,0,1:T(8,128)S(1)} %get-tuple-element.187), channel_id=1, source_target_pairs={{1,0},{2,1},{3,2},{5,4},{6,5},{7,6},{9,8},{10,9},{11,10},{13,12},{... | collective-permute-start | bytes 18440 | tf_op jit(solution)/shard_map/ppermute | solution.py:26
  158.5 3.6 %collective-permute-start.3 = (f32[12,2,512]{2,1,0:T(2,128)S(1)}, f32[12,2,512]{2,1,0:T(2,128)S(1)}, u32[]{:S(2)}, u32[]{:S(2)}) collective-permute-start(f32[12,2,512]{2,1,0:T(2,128)S(1)} %get-tuple-element.177), channel_id=1, source_target_pairs={{1,0},{2,1},{3,2},{5,4},{6,5},{7,6},{9,8},{10,9},{11,10},{13,12},{... | collective-permute-start | bytes 147464 | tf_op jit(solution)/shard_map/ppermute | solution.py:26
  164.6 10.7 %convolution_add_fusion.5 = f32[8,32,512]{2,1,0:T(8,128)S(1)} fusion(f32[8,32,256]{2,1,0:T(8,128)S(1)} %convolution_bitcast_fusion, f32[12,36,516]{2,1,0:T(8,128)S(1)} %select_maximum_fusion.4, f32[12,34,512]{2,1,0:T(8,128)S(1)} %get-tuple-element.175, f32[2,32,512]{2,1,0:T(8,128)S(1)} %collective-permute-done.1, f32[8,32,512]{2,1,0:T(8,128)S(1)} %bitcast.116, ...), kind=kOutput, calls=%fused_computation.282 | convolution fusion | flops 436600832 | bytes 64495616 | tf_op jit(solution)/shard_map/fc,abc->abf/dot_general | solution.py:91
  178.8 3.7 %collective-permute-start.20 = (f32[2,32,512]{2,1,0:T(8,128)S(1)}, f32[2,32,512]{2,1,0:T(8,128)S(1)}, u32[]{:S(2)}, u32[]{:S(2)}) collective-permute-start(f32[2,32,512]{2,1,0:T(8,128)S(1)} %get-tuple-element.179), channel_id=1, source_target_pairs={{4,0},{8,4},{12,8},{16,12},{20,16},{24,20},{28,24},{5,1},{9,5},{13... | collective-permute-start | bytes 393224 | tf_op jit(solution)/shard_map/ppermute | solution.py:26
  182.5 2.1 collective-permute-start.21
  184.6 2.4 collective-permute-done.20
  187.0 3.2 %collective-permute-done.21 = f32[2,32,512]{2,1,0:T(8,128)S(1)} collective-permute-done((f32[2,32,512]{2,1,0:T(8,128)S(1)}, f32[2,32,512]{2,1,0:T(8,128)S(1)}, u32[]{:S(2)}, u32[]{:S(2)}) %collective-permute-start.21) | collective-permute-done | bytes 131104 | tf_op jit(solution)/shard_map/ppermute | solution.py:24
  190.3 2.6 %collective-permute-start.22 = (f32[12,2,512]{2,1,0:T(2,128)S(1)}, f32[12,2,512]{2,1,0:T(2,128)S(1)}, u32[]{:S(2)}, u32[]{:S(2)}) collective-permute-start(f32[12,2,512]{2,1,0:T(2,128)S(1)} %get-tuple-element.173), channel_id=1, source_target_pairs={{1,0},{2,1},{3,2},{5,4},{6,5},{7,6},{9,8},{10,9},{11,10},{13,12},{... | collective-permute-start | bytes 147464 | tf_op jit(solution)/shard_map/ppermute | solution.py:26
  195.2 3.1 %collective-permute-done.23 = f32[12,2,512]{2,1,0:T(2,128)S(1)} collective-permute-done((f32[12,2,512]{2,1,0:T(2,128)S(1)}, f32[12,2,512]{2,1,0:T(2,128)S(1)}, u32[]{:S(2)}, u32[]{:S(2)}) %collective-permute-start.23) | collective-permute-done | bytes 49184 | tf_op jit(solution)/shard_map/ppermute | solution.py:24
  200.3 40.4 %while.26 = (s32[]{:T(128)}, f32[16,512,3]{1,2,0:T(4,128)}, f32[16,512]{1,0:T(8,128)S(1)}, s32[16,512]{1,0:T(8,128)S(1)}, f32[3,256,512]{1,2,0:T(8,128)S(1)}, /*index=5*/s32[16,512]{1,0:T(8,128)S(1)}, s32[]{:T(128)}) while((s32[]{:T(128)}, f32[16,512,3]{1,2,0:T(4,128)}, f32[16,512]{1,0:T(8,128)S(1)}, s32[16,512]{1,0:T(8,128)S(1)}, ...), condition=%wide.region_18.19_spmd.clone, body=%wide.region_16.18_spmd.clone.sunk | while | flops 2418147840 | bytes 3709525 | solution.py:256
  (272 shorter events, 92.2 us)
Async XLA Ops:
  75.7 26.8 %collective-permute-start.12 = (f32[2,8,128]{2,1,0:T(8,128)S(1)}, f32[2,8,128]{2,1,0:T(8,128)S(1)}, u32[]{:S(2)}, u32[]{:S(2)}) collective-permute-start(f32[2,8,128]{2,1,0:T(8,128)S(1)} %reduce_sum.100), channel_id=1, source_target_pairs={{0,4},{4,8},{8,12},{12,16},{16,20},{20,24},{24,28},{1,5},{5,9},{9,... | collective-permute-start | bytes 24584 | tf_op jit(solution)/shard_map/ppermute | solution.py:24
  79.1 23.4 %collective-permute-start.13 = (f32[2,8,128]{2,1,0:T(8,128)S(1)}, f32[2,8,128]{2,1,0:T(8,128)S(1)}, u32[]{:S(2)}, u32[]{:S(2)}) collective-permute-start(f32[2,8,128]{2,1,0:T(8,128)S(1)} %reduce_sum.100), channel_id=1, source_target_pairs={{4,0},{8,4},{12,8},{16,12},{20,16},{24,20},{28,24},{5,1},{9,5},{13... | collective-permute-start | bytes 24584 | tf_op jit(solution)/shard_map/ppermute | solution.py:26
  82.6 38.4 %collective-permute-start.4 = (f32[2,16,256]{2,0,1:T(2,128)S(1)}, f32[2,16,256]{2,0,1:T(2,128)S(1)}, u32[]{:S(2)}, u32[]{:S(2)}) collective-permute-start(f32[2,16,256]{2,0,1:T(2,128)S(1)} %get-tuple-element.190), channel_id=1, source_target_pairs={{0,4},{4,8},{8,12},{12,16},{16,20},{20,24},{24,28},{1,5},{5,9},{9,... | collective-permute-start | bytes 98312 | tf_op jit(solution)/shard_map/ppermute | solution.py:24
  85.1 39.6 %collective-permute-start.5 = (f32[2,16,256]{2,0,1:T(2,128)S(1)}, f32[2,16,256]{2,0,1:T(2,128)S(1)}, u32[]{:S(2)}, u32[]{:S(2)}) collective-permute-start(f32[2,16,256]{2,0,1:T(2,128)S(1)} %get-tuple-element.191), channel_id=1, source_target_pairs={{4,0},{8,4},{12,8},{16,12},{20,16},{24,20},{28,24},{5,1},{9,5},{13... | collective-permute-start | bytes 98312 | tf_op jit(solution)/shard_map/ppermute | solution.py:26
  89.3 67.2 %collective-permute-start = (f32[2,32,512]{2,1,0:T(8,128)S(1)}, f32[2,32,512]{2,1,0:T(8,128)S(1)}, u32[]{:S(2)}, u32[]{:S(2)}) collective-permute-start(f32[2,32,512]{2,1,0:T(8,128)S(1)} %bitcast.127), channel_id=1, source_target_pairs={{0,4},{4,8},{8,12},{12,16},{16,20},{20,24},{24,28},{1,5},{5,9},{9,... | collective-permute-start | bytes 393224 | tf_op jit(solution)/shard_map/ppermute | solution.py:24
  95.4 56.7 %all-to-all-start = ((f32[32,1,336]{2,1,0:T(1,128)}), f32[32,1,336]{2,1,0:T(1,128)S(1)}, u32[]{:S(2)}, u32[]{:S(2)}) async-start(f32[32,1,336]{2,1,0:T(1,128)} %stack.10), calls=%async_computation | async-start | bytes 98304 | tf_op jit(solution)/shard_map/all_to_all | solution.py:192
  102.5 5.6 %collective-permute-start.14 = (f32[6,2,128]{2,1,0:T(2,128)S(1)}, f32[6,2,128]{2,1,0:T(2,128)S(1)}, u32[]{:S(2)}, u32[]{:S(2)}) collective-permute-start(f32[6,2,128]{2,1,0:T(2,128)S(1)} %get-tuple-element.194), channel_id=1, source_target_pairs={{0,1},{1,2},{2,3},{4,5},{5,6},{6,7},{8,9},{9,10},{10,11},{12,13},{... | collective-permute-start | bytes 18440 | tf_op jit(solution)/shard_map/ppermute | solution.py:24
  104.5 4.9 %collective-permute-start.15 = (f32[6,2,128]{2,1,0:T(2,128)S(1)}, f32[6,2,128]{2,1,0:T(2,128)S(1)}, u32[]{:S(2)}, u32[]{:S(2)}) collective-permute-start(f32[6,2,128]{2,1,0:T(2,128)S(1)} %get-tuple-element.195), channel_id=1, source_target_pairs={{1,0},{2,1},{3,2},{5,4},{6,5},{7,6},{9,8},{10,9},{11,10},{13,12},{... | collective-permute-start | bytes 18440 | tf_op jit(solution)/shard_map/ppermute | solution.py:26
  109.8 6.8 %collective-permute-start.16 = (f32[1,8,128]{2,1,0:T(8,128)S(1)}, f32[1,8,128]{2,1,0:T(8,128)S(1)}, u32[]{:S(2)}, u32[]{:S(2)}) collective-permute-start(f32[1,8,128]{2,1,0:T(8,128)S(1)} %get-tuple-element.198), channel_id=1, source_target_pairs={{0,4},{4,8},{8,12},{12,16},{16,20},{20,24},{24,28},{1,5},{5,9},{9,... | collective-permute-start | bytes 12296 | tf_op jit(solution)/shard_map/ppermute | solution.py:24
  113.2 5.9 %collective-permute-start.17 = (f32[1,8,128]{2,1,0:T(8,128)S(1)}, f32[1,8,128]{2,1,0:T(8,128)S(1)}, u32[]{:S(2)}, u32[]{:S(2)}) collective-permute-start(f32[1,8,128]{2,1,0:T(8,128)S(1)} %get-tuple-element.199), channel_id=1, source_target_pairs={{4,0},{8,4},{12,8},{16,12},{20,16},{24,20},{28,24},{5,1},{9,5},{13... | collective-permute-start | bytes 12296 | tf_op jit(solution)/shard_map/ppermute | solution.py:26
  116.6 39.9 %collective-permute-start.1 = (f32[2,32,512]{2,1,0:T(8,128)S(1)}, f32[2,32,512]{2,1,0:T(8,128)S(1)}, u32[]{:S(2)}, u32[]{:S(2)}) collective-permute-start(f32[2,32,512]{2,1,0:T(8,128)S(1)} %bitcast.126), channel_id=1, source_target_pairs={{4,0},{8,4},{12,8},{16,12},{20,16},{24,20},{28,24},{5,1},{9,5},{13... | collective-permute-start | bytes 393224 | tf_op jit(solution)/shard_map/ppermute | solution.py:26
  119.1 7.6 %collective-permute-start.18 = (f32[4,1,128]{2,1,0:T(1,128)S(1)}, f32[4,1,128]{2,1,0:T(1,128)S(1)}, u32[]{:S(2)}, u32[]{:S(2)}) collective-permute-start(f32[4,1,128]{2,1,0:T(1,128)S(1)} %get-tuple-element.196), channel_id=1, source_target_pairs={{0,1},{1,2},{2,3},{4,5},{5,6},{6,7},{8,9},{9,10},{10,11},{12,13},{... | collective-permute-start | bytes 6152 | tf_op jit(solution)/shard_map/ppermute | solution.py:24
  121.0 9.3 %collective-permute-start.19 = (f32[4,1,128]{2,1,0:T(1,128)S(1)}, f32[4,1,128]{2,1,0:T(1,128)S(1)}, u32[]{:S(2)}, u32[]{:S(2)}) collective-permute-start(f32[4,1,128]{2,1,0:T(1,128)S(1)} %get-tuple-element.197), channel_id=1, source_target_pairs={{1,0},{2,1},{3,2},{5,4},{6,5},{7,6},{9,8},{10,9},{11,10},{13,12},{... | collective-permute-start | bytes 6152 | tf_op jit(solution)/shard_map/ppermute | solution.py:26
  124.7 5.6 %collective-permute-start.6 = (f32[8,2,256]{2,0,1:T(8,128)S(1)}, f32[8,2,256]{2,0,1:T(8,128)S(1)}, u32[]{:S(2)}, u32[]{:S(2)}) collective-permute-start(f32[8,2,256]{2,0,1:T(8,128)S(1)} %get-tuple-element.184), channel_id=1, source_target_pairs={{0,1},{1,2},{2,3},{4,5},{5,6},{6,7},{8,9},{9,10},{10,11},{12,13},{... | collective-permute-start | bytes 49160 | tf_op jit(solution)/shard_map/ppermute | solution.py:24
  126.6 5.1 %collective-permute-start.7 = (f32[8,2,256]{2,0,1:T(8,128)S(1)}, f32[8,2,256]{2,0,1:T(8,128)S(1)}, u32[]{:S(2)}, u32[]{:S(2)}) collective-permute-start(f32[8,2,256]{2,0,1:T(8,128)S(1)} %get-tuple-element.185), channel_id=1, source_target_pairs={{1,0},{2,1},{3,2},{5,4},{6,5},{7,6},{9,8},{10,9},{11,10},{13,12},{... | collective-permute-start | bytes 49160 | tf_op jit(solution)/shard_map/ppermute | solution.py:26
  134.8 7.0 %collective-permute-start.8 = (f32[1,16,256]{2,0,1:T(1,128)S(1)}, f32[1,16,256]{2,0,1:T(1,128)S(1)}, u32[]{:S(2)}, u32[]{:S(2)}) collective-permute-start(f32[1,16,256]{2,0,1:T(1,128)S(1)} %get-tuple-element.188), channel_id=1, source_target_pairs={{0,4},{4,8},{8,12},{12,16},{16,20},{20,24},{24,28},{1,5},{5,9},{9,... | collective-permute-start | bytes 49160 | tf_op jit(solution)/shard_map/ppermute | solution.py:24
  138.7 5.6 %collective-permute-start.9 = (f32[1,16,256]{2,0,1:T(1,128)S(1)}, f32[1,16,256]{2,0,1:T(1,128)S(1)}, u32[]{:S(2)}, u32[]{:S(2)}) collective-permute-start(f32[1,16,256]{2,0,1:T(1,128)S(1)} %get-tuple-element.189), channel_id=1, source_target_pairs={{4,0},{8,4},{12,8},{16,12},{20,16},{24,20},{28,24},{5,1},{9,5},{13... | collective-permute-start | bytes 49160 | tf_op jit(solution)/shard_map/ppermute | solution.py:26
  144.4 6.1 %collective-permute-start.10 = (f32[6,1,256]{2,0,1:T(8,128)S(1)}, f32[6,1,256]{2,0,1:T(8,128)S(1)}, u32[]{:S(2)}, u32[]{:S(2)}) collective-permute-start(f32[6,1,256]{2,0,1:T(8,128)S(1)} %get-tuple-element.186), channel_id=1, source_target_pairs={{0,1},{1,2},{2,3},{4,5},{5,6},{6,7},{8,9},{9,10},{10,11},{12,13},{... | collective-permute-start | bytes 18440 | tf_op jit(solution)/shard_map/ppermute | solution.py:24
  146.3 5.0 %collective-permute-start.11 = (f32[6,1,256]{2,0,1:T(8,128)S(1)}, f32[6,1,256]{2,0,1:T(8,128)S(1)}, u32[]{:S(2)}, u32[]{:S(2)}) collective-permute-start(f32[6,1,256]{2,0,1:T(8,128)S(1)} %get-tuple-element.187), channel_id=1, source_target_pairs={{1,0},{2,1},{3,2},{5,4},{6,5},{7,6},{9,8},{10,9},{11,10},{13,12},{... | collective-permute-start | bytes 18440 | tf_op jit(solution)/shard_map/ppermute | solution.py:26
  156.6 5.9 %collective-permute-start.2 = (f32[12,2,512]{2,1,0:T(2,128)S(1)}, f32[12,2,512]{2,1,0:T(2,128)S(1)}, u32[]{:S(2)}, u32[]{:S(2)}) collective-permute-start(f32[12,2,512]{2,1,0:T(2,128)S(1)} %get-tuple-element.176), channel_id=1, source_target_pairs={{0,1},{1,2},{2,3},{4,5},{5,6},{6,7},{8,9},{9,10},{10,11},{12,13},{... | collective-permute-start | bytes 147464 | tf_op jit(solution)/shard_map/ppermute | solution.py:24
  158.5 5.4 %collective-permute-start.3 = (f32[12,2,512]{2,1,0:T(2,128)S(1)}, f32[12,2,512]{2,1,0:T(2,128)S(1)}, u32[]{:S(2)}, u32[]{:S(2)}) collective-permute-start(f32[12,2,512]{2,1,0:T(2,128)S(1)} %get-tuple-element.177), channel_id=1, source_target_pairs={{1,0},{2,1},{3,2},{5,4},{6,5},{7,6},{9,8},{10,9},{11,10},{13,12},{... | collective-permute-start | bytes 147464 | tf_op jit(solution)/shard_map/ppermute | solution.py:26
  178.7 20.2 %copy-start = (f32[8,32,512]{2,1,0:T(8,128)}, f32[8,32,512]{2,1,0:T(8,128)S(1)}, u32[]{:S(2)}) copy-start(f32[8,32,512]{2,1,0:T(8,128)S(1)} %convolution_add_fusion.1) | copy-start | bytes 1572868
  178.8 8.3 %collective-permute-start.20 = (f32[2,32,512]{2,1,0:T(8,128)S(1)}, f32[2,32,512]{2,1,0:T(8,128)S(1)}, u32[]{:S(2)}, u32[]{:S(2)}) collective-permute-start(f32[2,32,512]{2,1,0:T(8,128)S(1)} %get-tuple-element.179), channel_id=1, source_target_pairs={{4,0},{8,4},{12,8},{16,12},{20,16},{24,20},{28,24},{5,1},{9,5},{13... | collective-permute-start | bytes 393224 | tf_op jit(solution)/shard_map/ppermute | solution.py:26
  182.5 7.8 %collective-permute-start.21 = (f32[2,32,512]{2,1,0:T(8,128)S(1)}, f32[2,32,512]{2,1,0:T(8,128)S(1)}, u32[]{:S(2)}, u32[]{:S(2)}) collective-permute-start(f32[2,32,512]{2,1,0:T(8,128)S(1)} %get-tuple-element.178), channel_id=1, source_target_pairs={{0,4},{4,8},{8,12},{12,16},{16,20},{20,24},{24,28},{1,5},{5,9},{9,... | collective-permute-start | bytes 393224 | tf_op jit(solution)/shard_map/ppermute | solution.py:24
  190.3 4.8 %collective-permute-start.22 = (f32[12,2,512]{2,1,0:T(2,128)S(1)}, f32[12,2,512]{2,1,0:T(2,128)S(1)}, u32[]{:S(2)}, u32[]{:S(2)}) collective-permute-start(f32[12,2,512]{2,1,0:T(2,128)S(1)} %get-tuple-element.173), channel_id=1, source_target_pairs={{1,0},{2,1},{3,2},{5,4},{6,5},{7,6},{9,8},{10,9},{11,10},{13,12},{... | collective-permute-start | bytes 147464 | tf_op jit(solution)/shard_map/ppermute | solution.py:26
  192.9 5.4 %collective-permute-start.23 = (f32[12,2,512]{2,1,0:T(2,128)S(1)}, f32[12,2,512]{2,1,0:T(2,128)S(1)}, u32[]{:S(2)}, u32[]{:S(2)}) collective-permute-start(f32[12,2,512]{2,1,0:T(2,128)S(1)} %get-tuple-element.172), channel_id=1, source_target_pairs={{0,1},{1,2},{2,3},{4,5},{5,6},{6,7},{8,9},{9,10},{10,11},{12,13},{... | collective-permute-start | bytes 147464 | tf_op jit(solution)/shard_map/ppermute | solution.py:24
